TPU v7x, 32 devices: a whole 2x2x4 slice. The times are simulated.
32 devices in a mesh: section: 2 (over y), dp: 16 (over z, x, core).
Axes of the slice: x: 2, y: 2, z: 4, core: 2. Of those that a mesh axis runs over, the one named last changes fastest.
Arguments:
- inputs: bfloat16 [4096, 768], P('dp'), may hold values from -6 to 6
- cotangent: bfloat16 [4096, 768], P('dp'), may hold values from -6 to 6
- segments: int32 [4096], P('dp'), may hold values from 0 to 3, as said below
- qkv_weight: bfloat16 [2, 768, 2304], P('section', 'dp'), may hold values from -0.21875 to 0.21875
- out_weight: bfloat16 [2, 768, 768], P('section', 'dp'), may hold values from -0.875 to 0.875
- up_weight: bfloat16 [2, 768, 3072], P('section', 'dp'), may hold values from -0.21875 to 0.21875
- down_weight: bfloat16 [2, 3072, 768], P('section', 'dp'), may hold values from -0.109375 to 0.109375
- norm_params: bfloat16 [2, 4, 768], P('section', None, 'dp'), may hold values from 0.5 to 1.5
- bias_params: bfloat16 [2, 4, 768], P('section', None, 'dp'), may hold values from -3 to 3
- up_bias: bfloat16 [2, 3072], P('section', 'dp'), may hold values from -3 to 3
Outputs:
- layer_outputs: bfloat16 [2, 4096, 768], P('section', 'dp')
- input_grads: bfloat16 [2, 4096, 768], P('section', 'dp')
- qkv_grad: float32 [2, 768, 2304], P('section', 'dp')
- out_grad: float32 [2, 768, 768], P('section', 'dp')
- up_grad: float32 [2, 768, 3072], P('section', 'dp')
- down_grad: float32 [2, 3072, 768], P('section', 'dp')
- norm_grad: float32 [2, 4, 768], P('section', None, 'dp')
- bias_grad: float32 [2, 4, 768], P('section', None, 'dp')
- up_bias_grad: float32 [2, 3072], P('section', 'dp')
Inputs may be any that keep to these rules, and one draw needn't show every extreme that they name: `segments`: within each aligned block of 128 positions the numbers start at 0 and rise by one where a new sequence starts; every block holds exactly 4 sequences; no sequence crosses a block.
All inputs are finite; a program needn't handle non-finite values.
Results may differ from a plain program's by a relative error of at most 0.014.
Values may be sent and summed in bfloat16 or wider, within the bound.
A program may use at most 256 MiB of HBM per device.

v0:
```python
import math

import jax
import jax.numpy as jnp
from jax import lax
from jax.sharding import PartitionSpec as P

D = 768
FF = 3072
HEAD = 64
ROT = 16
MICRO = 2


EPS = 1e-05
HALF_ROOT = 0.7071067811865476
INV_ROOT_TAU = 0.3989422804014327
NEGATIVE = -1e30


def shifted(value, axis, steps):
    count = lax.axis_size(axis)
    initial, last = (max(0, -steps), min(count, count - steps))
    return lax.ppermute(value, axis, [(source, source + steps) for source in range(initial, last)])


def mix(form, left, right):
    return jnp.einsum(form, left, right, preferred_element_type=jnp.float32)


def layer_normalize(input_float, norm_gain, norm_shift):
    row_mean = jnp.mean(input_float, axis=-1, keepdims=True)
    centered_input = input_float - row_mean
    inverse_deviation = lax.rsqrt(
        jnp.mean(centered_input * centered_input, axis=-1, keepdims=True) + EPS
    )
    standardized_input = centered_input * inverse_deviation
    return (
        standardized_input,
        inverse_deviation,
        (standardized_input * norm_gain + norm_shift).astype(jnp.bfloat16),
    )


def layer_normalize_backward(normed_gradient, standardized_input, inverse_deviation, norm_gain):
    standardized_gradient = normed_gradient * norm_gain
    inner_width = jnp.mean(
        standardized_gradient, axis=-1, keepdims=True
    ) + standardized_input * jnp.mean(
        standardized_gradient * standardized_input, axis=-1, keepdims=True
    )
    return (
        inverse_deviation * (standardized_gradient - inner_width),
        jnp.sum(normed_gradient * standardized_input, axis=0),
        jnp.sum(normed_gradient, axis=0),
    )


def rotary_tables(seg):
    width = seg.shape[1]
    index = jnp.arange(width, dtype=jnp.int32)[None, :]
    before = jnp.concatenate([seg[:, :1] - 1, seg[:, :-1]], axis=1)
    first = lax.cummax(jnp.where(seg != before, index, 0), axis=1)
    place = (index - first).astype(jnp.float32)
    freq = 10000.0 ** (-jnp.arange(0, ROT, 2, dtype=jnp.float32) / ROT)
    angle = place[:, :, None, None] * freq
    return (jnp.cos(angle), jnp.sin(angle))


def rotate(tensor, cosine, sine, sign):
    half = ROT // 2
    first = tensor[..., :half]
    second = tensor[..., half:ROT]
    return jnp.concatenate(
        [
            first * cosine - sign * second * sine,
            second * cosine + sign * first * sine,
            tensor[..., ROT:],
        ],
        axis=-1,
    )


def scores(query_rows, key_rows, seg):
    width = seg.shape[1]
    raw = mix("prhe,pshe->phrs", query_rows, key_rows) * (1.0 / math.sqrt(HEAD))
    index = jnp.arange(width, dtype=jnp.int32)
    causal = index[:, None] >= index[None, :]
    allowed = (seg[:, None, :, None] == seg[:, None, None, :]) & causal[None, None]
    return jnp.where(allowed, raw, NEGATIVE)


def forward(x, seg, weights):
    wqkv, wout, wup, wdown, norm_pairs, abias, upbias = weights
    packs, width = seg.shape
    shape = (packs, width, D // HEAD, HEAD)
    norm_pairs = norm_pairs.astype(jnp.float32)
    abias = abias.astype(jnp.float32)
    upbias = upbias.astype(jnp.float32)
    input_float = x.astype(jnp.float32)
    first_standardized, first_inverse_deviation, first_normed = layer_normalize(
        input_float, norm_pairs[0], norm_pairs[1]
    )
    second_standardized, second_inverse_deviation, second_normed = layer_normalize(
        input_float, norm_pairs[2], norm_pairs[3]
    )
    qkv = jnp.dot(first_normed, wqkv, preferred_element_type=jnp.float32)
    cosine, sine = rotary_tables(seg)
    query_rows = rotate((qkv[:, :D] + abias[0]).reshape(shape), cosine, sine, 1.0).astype(
        jnp.bfloat16
    )
    key_rows = rotate(qkv[:, D : 2 * D].reshape(shape), cosine, sine, 1.0).astype(jnp.bfloat16)
    value_rows = (qkv[:, 2 * D :] + abias[1]).reshape(shape).astype(jnp.bfloat16)
    raw = scores(query_rows, key_rows, seg)
    top = jnp.max(raw, axis=-1, keepdims=True)
    log_sum_exp = top + jnp.log(jnp.sum(jnp.exp(raw - top), axis=-1, keepdims=True))
    probs = jnp.exp(raw - log_sum_exp).astype(jnp.bfloat16)
    context_rows = (
        mix("phrs,pshe->prhe", probs, value_rows).reshape(packs * width, D).astype(jnp.bfloat16)
    )
    attended = jnp.dot(context_rows, wout, preferred_element_type=jnp.float32) + abias[2]
    hidden_rows = jnp.dot(second_normed, wup, preferred_element_type=jnp.float32) + upbias
    activation_output = (0.5 * hidden_rows * (1.0 + lax.erf(hidden_rows * HALF_ROOT))).astype(
        jnp.bfloat16
    )
    mlp = jnp.dot(activation_output, wdown, preferred_element_type=jnp.float32) + abias[3]
    result = (input_float + attended + mlp).astype(jnp.bfloat16)
    saved_state = (
        first_standardized,
        first_inverse_deviation,
        first_normed,
        second_standardized,
        second_inverse_deviation,
        second_normed,
        query_rows,
        key_rows,
        value_rows,
        log_sum_exp,
        context_rows,
        hidden_rows,
        activation_output,
    )
    return (result, saved_state)


def blank_forward(rows):
    heads = D // HEAD
    single = jnp.float32
    half = jnp.bfloat16
    saved_state = (
        jnp.zeros((rows, D), single),
        jnp.zeros((rows, 1), single),
        jnp.zeros((rows, D), half),
        jnp.zeros((rows, D), single),
        jnp.zeros((rows, 1), single),
        jnp.zeros((rows, D), half),
        jnp.zeros((1, rows, heads, HEAD), half),
        jnp.zeros((1, rows, heads, HEAD), half),
        jnp.zeros((1, rows, heads, HEAD), half),
        jnp.zeros((1, heads, rows, 1), single),
        jnp.zeros((rows, D), half),
        jnp.zeros((rows, FF), single),
        jnp.zeros((rows, FF), half),
    )
    return (jnp.zeros((rows, D), half), saved_state)


def backward(saved_state, upstream, seg, weights):
    wqkv, wout, wup, wdown, norm_pairs, abias, upbias = weights
    (
        first_standardized,
        first_inverse_deviation,
        first_normed,
        second_standardized,
        second_inverse_deviation,
        second_normed,
        query_rows,
        key_rows,
        value_rows,
        log_sum_exp,
        context_rows,
        hidden_rows,
        activation_output,
    ) = saved_state
    packs, width = seg.shape
    shape = (packs, width, D // HEAD, HEAD)
    norm_pairs = norm_pairs.astype(jnp.float32)
    upf = upstream.astype(jnp.float32)
    d_down = jnp.dot(activation_output.T, upstream, preferred_element_type=jnp.float32)
    dgelu = jnp.dot(upstream, wdown.T, preferred_element_type=jnp.float32)
    slope = 0.5 * (1.0 + lax.erf(hidden_rows * HALF_ROOT)) + hidden_rows * INV_ROOT_TAU * jnp.exp(
        -0.5 * hidden_rows * hidden_rows
    )
    dhidden = dgelu * slope
    dhidden_low = dhidden.astype(jnp.bfloat16)
    d_up = jnp.dot(second_normed.T, dhidden_low, preferred_element_type=jnp.float32)
    second_norm_gradient = jnp.dot(dhidden_low, wup.T, preferred_element_type=jnp.float32)
    d_out = jnp.dot(context_rows.T, upstream, preferred_element_type=jnp.float32)
    dctx = (
        jnp.dot(upstream, wout.T, preferred_element_type=jnp.float32)
        .reshape(shape)
        .astype(jnp.bfloat16)
    )
    probs = jnp.exp(scores(query_rows, key_rows, seg) - log_sum_exp)
    dvalues = mix("phrs,prhe->pshe", probs.astype(jnp.bfloat16), dctx)
    dprobs = mix("prhe,pshe->phrs", dctx, value_rows)
    dscores = (
        probs * (dprobs - jnp.sum(probs * dprobs, axis=-1, keepdims=True)) * (1.0 / math.sqrt(HEAD))
    ).astype(jnp.bfloat16)
    dquery = mix("phrs,pshe->prhe", dscores, key_rows)
    dkeys = mix("phrs,prhe->pshe", dscores, query_rows)
    cosine, sine = rotary_tables(seg)
    dquery = rotate(dquery, cosine, sine, -1.0).reshape(packs * width, D)
    dkeys = rotate(dkeys, cosine, sine, -1.0).reshape(packs * width, D)
    dvalues = dvalues.reshape(packs * width, D)
    dqkv = jnp.concatenate([dquery, dkeys, dvalues], axis=1).astype(jnp.bfloat16)
    d_qkv = jnp.dot(first_normed.T, dqkv, preferred_element_type=jnp.float32)
    first_norm_gradient = jnp.dot(dqkv, wqkv.T, preferred_element_type=jnp.float32)
    first_input_gradient, first_gain_gradient, first_shift_gradient = layer_normalize_backward(
        first_norm_gradient, first_standardized, first_inverse_deviation, norm_pairs[0]
    )
    second_input_gradient, second_gain_gradient, second_shift_gradient = layer_normalize_backward(
        second_norm_gradient, second_standardized, second_inverse_deviation, norm_pairs[2]
    )
    grad_in = (upf + first_input_gradient + second_input_gradient).astype(jnp.bfloat16)
    d_norm = jnp.stack(
        [first_gain_gradient, first_shift_gradient, second_gain_gradient, second_shift_gradient]
    )
    column = jnp.sum(upf, axis=0)
    d_bias = jnp.stack([jnp.sum(dquery, axis=0), jnp.sum(dvalues, axis=0), column, column])
    d_upbias = jnp.sum(dhidden, axis=0)
    return (grad_in, (d_qkv, d_out, d_up, d_down, d_norm, d_bias, d_upbias))


def blank_backward(rows, weights):
    grads = tuple((jnp.zeros(piece.shape, jnp.float32) for piece in weights))
    return (jnp.zeros((rows, D), jnp.bfloat16), grads)


def forward_step(active, x_now, seg, weights):
    if active is None:
        return forward(x_now, seg, weights)
    return lax.cond(
        active, lambda: forward(x_now, seg, weights), lambda: blank_forward(x_now.shape[0])
    )


def backward_step(active, saved_state, upstream, seg, weights):
    if active is None:
        return backward(saved_state, upstream, seg, weights)
    return lax.cond(
        active,
        lambda: backward(saved_state, upstream, seg, weights),
        lambda: blank_backward(upstream.shape[0], weights),
    )


def send_forward(result):
    return shifted(result, "section", 1)


def send_back(grad_in):
    return shifted(grad_in, "section", -1)


def on_device(
    inputs,
    cotangent,
    segments,
    qkv_weight,
    out_weight,
    up_weight,
    down_weight,
    norm_params,
    bias_params,
    up_bias,
):
    is_first = lax.axis_index("section") == 0
    is_second = jnp.logical_not(is_first)
    micro = MICRO
    pack = inputs.shape[0] // micro
    gathered = (
        lax.all_gather(qkv_weight, "dp", axis=1, tiled=True),
        lax.all_gather(out_weight, "dp", axis=1, tiled=True),
        lax.all_gather(up_weight, "dp", axis=1, tiled=True),
        lax.all_gather(down_weight, "dp", axis=1, tiled=True),
        lax.all_gather(norm_params, "dp", axis=2, tiled=True),
        lax.all_gather(bias_params, "dp", axis=2, tiled=True),
        lax.all_gather(up_bias, "dp", axis=1, tiled=True),
    )
    weights = tuple((piece[0] for piece in gathered))

    def rows_of(array, index):
        return array[index * pack : (index + 1) * pack]

    arrived = jnp.zeros((pack, D), jnp.bfloat16)
    outs = []
    kept = []
    seg_list = []
    for step in range(micro + 1):
        lead = min(step, micro - 1)
        trail = max(step - 1, 0)
        x_now = jnp.where(is_first, rows_of(inputs, lead), arrived)
        seg = jnp.where(is_first, rows_of(segments, lead), rows_of(segments, trail)).reshape(
            1, pack
        )
        active = is_first if step == 0 else is_second if step == micro else None
        result, saved_state = forward_step(active, x_now, seg, weights)
        if step < micro:
            arrived = send_forward(result)
        outs.append(result)
        kept.append(saved_state)
        seg_list.append(seg)
    regathered = (
        lax.all_gather(qkv_weight, "dp", axis=1, tiled=True),
        lax.all_gather(out_weight, "dp", axis=1, tiled=True),
        lax.all_gather(up_weight, "dp", axis=1, tiled=True),
        lax.all_gather(down_weight, "dp", axis=1, tiled=True),
        lax.all_gather(norm_params, "dp", axis=2, tiled=True),
        lax.all_gather(bias_params, "dp", axis=2, tiled=True),
        lax.all_gather(up_bias, "dp", axis=1, tiled=True),
    )
    back_weights = tuple((piece[0] for piece in regathered))
    returned = jnp.zeros((pack, D), jnp.bfloat16)
    grads_in = []
    total = None
    owned = None
    for step in range(micro + 1):
        index = micro - step
        upstream = jnp.where(is_first, returned, rows_of(cotangent, max(micro - 1 - step, 0)))
        active = is_second if step == 0 else is_first if step == micro else None
        grad_in, grads = backward_step(active, kept[index], upstream, seg_list[index], back_weights)
        if step < micro:
            returned = send_back(grad_in)
        grads_in.append(grad_in)
        total = (
            grads if total is None else tuple((left + right for left, right in zip(total, grads)))
        )
    owned = (
        lax.psum_scatter(total[0][None], "dp", scatter_dimension=1, tiled=True),
        lax.psum_scatter(total[1][None], "dp", scatter_dimension=1, tiled=True),
        lax.psum_scatter(total[2][None], "dp", scatter_dimension=1, tiled=True),
        lax.psum_scatter(total[3][None], "dp", scatter_dimension=1, tiled=True),
        lax.psum_scatter(total[4][None], "dp", scatter_dimension=2, tiled=True),
        lax.psum_scatter(total[5][None], "dp", scatter_dimension=2, tiled=True),
        lax.psum_scatter(total[6][None], "dp", scatter_dimension=1, tiled=True),
    )
    layer_out = jnp.concatenate(
        [jnp.where(is_first, outs[j], outs[j + 1]) for j in range(micro)], axis=0
    )
    input_grad = jnp.concatenate(
        [jnp.where(is_first, grads_in[micro - j], grads_in[micro - 1 - j]) for j in range(micro)],
        axis=0,
    )
    return (
        layer_out[None],
        input_grad[None],
        owned[0],
        owned[1],
        owned[2],
        owned[3],
        owned[4],
        owned[5],
        owned[6],
    )


def solution(mesh):
    in_specs = (
        P("dp", None),
        P("dp", None),
        P("dp"),
        P("section", "dp", None),
        P("section", "dp", None),
        P("section", "dp", None),
        P("section", "dp", None),
        P("section", None, "dp"),
        P("section", None, "dp"),
        P("section", "dp"),
    )
    out_specs = (
        P("section", "dp", None),
        P("section", "dp", None),
        P("section", "dp", None),
        P("section", "dp", None),
        P("section", "dp", None),
        P("section", "dp", None),
        P("section", None, "dp"),
        P("section", None, "dp"),
        P("section", "dp"),
    )
    return jax.shard_map(
        on_device, mesh=mesh, in_specs=in_specs, out_specs=out_specs, check_vma=False
    )
```

profile of v0, /device:TPU:0, one launch (start us, length us, event | category | flops | bytes accessed | tf_op | source)
XLA Modules:
  0.0 1064.7 jit_solution(13864826824527984078)
XLA Ops:
  10.9 24.3 %all_gather.26 = bf16[1,4,768]{1,0,2:T(2,128)(2,1)S(1)} all-gather(bf16[1,4,48]{1,0,2:T(2,128)(2,1)S(1)} %copy.194), channel_id=1, replica_groups=mesh['section'=2,'dp'=16] {'dp'}, dimensions={2}, use_global_device_ids=true | all-gather | bytes 6528 | tf_op jit(solution)/shard_map/all_gather | solution.py:287
  35.6 19.4 %all_gather.28 = bf16[1,4,768]{1,0,2:T(2,128)(2,1)S(1)} all-gather(bf16[1,4,48]{1,0,2:T(2,128)(2,1)S(1)} %copy.196), channel_id=1, replica_groups=mesh['section'=2,'dp'=16] {'dp'}, dimensions={2}, use_global_device_ids=true | all-gather | bytes 6528 | tf_op jit(solution)/shard_map/all_gather | solution.py:288
  56.8 32.1 %all-reduce = bf16[3072]{0:T(1024)(128)(2,1)S(1)} all-reduce(bf16[3072]{0:T(1024)(128)(2,1)S(1)} %dynamic-update-slice), channel_id=1, replica_groups=mesh['section'=2,'dp'=16] {'dp'}, use_global_device_ids=true, to_apply=%add | all-reduce | flops 3072 | bytes 12288 | tf_op jit(solution)/shard_map/squeeze | solution.py:291
  92.0 8.3 all-gather.5.cloned.1.call-done
  100.4 54.1 %all-gather.9.cloned.1.call-done = bf16[1,768,3072]{2,1,0:T(8,128)(2,1)} async-done(((bf16[1,48,3072]{2,1,0:T(8,128)(2,1)}), bf16[1,768,3072]{2,1,0:T(8,128)(2,1)}) %all-gather.9.cloned.1.call-update) | async-done | bytes 4718608 | tf_op jit(solution)/shard_map/all_gather | solution.py:285
  154.5 53.8 %all-gather.11.cloned.1.call-done = bf16[1,3072,768]{2,1,0:T(8,128)(2,1)} async-done(((bf16[1,192,768]{2,1,0:T(8,128)(2,1)}), bf16[1,3072,768]{2,1,0:T(8,128)(2,1)}) %all-gather.11.cloned.1.call-update) | async-done | bytes 4718608 | tf_op jit(solution)/shard_map/all_gather | solution.py:286
  209.0 14.8 %conditional.4 = (bf16[128,768]{1,0:T(8,128)(2,1)S(1)}, f32[128,768]{1,0:T(8,128)S(1)}, f32[128,1]{0,1:T(1,128)S(1)}, bf16[128,768]{1,0:T(8,128)(2,1)}, bf16[128...) conditional(s32[]{:T(128)} %convert_element_type.388, () %tuple.48, ...), branch_computations={%region_0.1_spmd, %region_1.7_spmd} | conditional | flops 1871193216 | bytes 78593992 | solution.py:243
  209.7 4.8 multiply_convert_fusion
  225.8 4.1 collective-permute-done
  231.3 2.7 fusion.218
  235.7 3.6 convolution_add_fusion.6
  242.2 5.1 collective-permute-start.1
  248.0 2.9 collective-permute-done.1
  250.9 8.2 conditional.5
  259.8 16.5 %conditional.6 = (bf16[128,768]{1,0:T(8,128)(2,1)}, f32[4,768]{1,0:T(4,128)}, f32[4,768]{1,0:T(4,128)}, f32[3072]{0:T(1024)}, f32[768,2304]{1,0:T(8,128)}, /*ind...) conditional(s32[]{:T(128)} %convert_element_type.404, () %tuple.53, (pred[]{:T(512)}, ...), branch_computations={%region_19.20_spmd, %region_20.35_spmd} | conditional | flops 3765398016 | bytes 151518880 | solution.py:251
  262.3 3.3 broadcast.876.clone
  267.2 4.8 broadcast.878.clone
  272.0 4.3 broadcast.879.clone
  279.6 96.0 %collective-permute-done.2 = bf16[128,768]{1,0:T(8,128)(2,1)S(1)} collective-permute-done((bf16[128,768]{1,0:T(8,128)(2,1)}, bf16[128,768]{1,0:T(8,128)(2,1)S(1)}, u32[]{:S(2)}, u32[]{:S(2)}) %collective-permute-start.2) | collective-permute-done | bytes 196640 | tf_op jit(solution)/shard_map/ppermute | solution.py:24
  379.4 3.2 convolution_bitcast_fusion.15
  382.6 3.2 convolution_bitcast_fusion.16
  389.0 4.8 fusion.240
  404.4 1.9 fusion.244
  406.4 84.0 %conditional.7 = (bf16[128,768]{1,0:T(8,128)(2,1)}, f32[4,768]{1,0:T(4,128)S(1)}, f32[4,768]{1,0:T(4,128)S(1)}, f32[3072]{0:T(1024)S(1)}, f32[768,2304]{1,0:T(8,...) conditional(s32[]{:T(128)} %convert_element_type.388, () %tuple.52, (pred[]{:T(512)}, ...), branch_computations={%region_40.41_spmd, %region_41.56_spmd} | conditional | flops 3765398016 | bytes 179386496 | solution.py:251
  407.3 5.6 fusion.237
  412.9 2.4 fusion.107
  420.5 2.0 convolution_bitcast_fusion.11
  422.5 1.8 slice.395
  433.2 3.1 convolution_bitcast_fusion.13
  439.5 2.8 multiply_reduce_fusion.9
  445.1 4.0 convolution_bitcast_fusion.9
  449.1 8.0 copy.245
  458.5 2.1 copy.247
  460.6 5.0 convolution_bitcast_fusion.8
  465.7 9.7 copy.249
  475.4 5.0 convolution_bitcast_fusion.7
  480.5 9.7 copy.251
  496.9 4.3 add_bitcast_fusion.3
  502.4 4.1 fusion.188
  506.5 11.2 %add_bitcast_fusion.2 = f32[1,768,2304]{2,1,0:T(8,128)} fusion(f32[768,2304]{1,0:T(8,128)} %get-tuple-element.661, f32[768,2304]{1,0:T(8,128)} %get-tuple-element.657, f32[768,2304]{1,0:T(8,128)} %fusion.188), kind=kLoop, calls=%fused_computation.291 | loop fusion | flops 3538944 | bytes 28311552 | tf_op jit(solution)/shard_map/broadcast_in_dim | solution.py:340
  520.4 10.9 %add_bitcast_fusion.1 = f32[1,768,3072]{2,1,0:T(8,128)} fusion(f32[768,3072]{1,0:T(8,128)} %get-tuple-element.663, f32[768,3072]{1,0:T(8,128)} %get-tuple-element.659, f32[768,3072]{1,0:T(8,128)S(1)} %fusion.176), kind=kLoop, calls=%fused_computation.290 | loop fusion | flops 4718592 | bytes 37748736 | tf_op jit(solution)/shard_map/broadcast_in_dim | solution.py:342
  534.2 11.0 %add_bitcast_fusion = f32[1,3072,768]{2,1,0:T(8,128)} fusion(f32[3072,768]{1,0:T(8,128)} %get-tuple-element.664, f32[3072,768]{1,0:T(8,128)} %get-tuple-element.660, f32[3072,768]{1,0:T(8,128)S(1)} %fusion.226), kind=kLoop, calls=%fused_computation.289 | loop fusion | flops 4718592 | bytes 37748736 | tf_op jit(solution)/shard_map/broadcast_in_dim | solution.py:343
  551.0 53.4 %reduce-scatter.24.cloned.1.call-done = f32[48,4]{1,0:T(8,128)} async-done(((f32[768,4]{1,0:T(8,128)}), f32[48,4]{1,0:T(8,128)}) %reduce-scatter.24.cloned.1.call-update) | async-done | bytes 784
  605.8 60.9 %reduce-scatter.26.cloned.1.call-done = f32[192,1]{1,0:T(8,128)} async-done(((f32[3072,1]{1,0:T(8,128)}), f32[192,1]{1,0:T(8,128)}) %reduce-scatter.26.cloned.1.call-update) | async-done | bytes 784
  668.2 65.0 %reduce-scatter.16.cloned.1.call-done = f32[1,48,768]{2,1,0:T(8,128)} async-done(((f32[1,768,768]{2,1,0:T(8,128)}), f32[1,48,768]{2,1,0:T(8,128)}) %reduce-scatter.16.cloned.1.call-update) | async-done | bytes 147472 | tf_op jit(solution)/shard_map/reduce_scatter | solution.py:341
  733.2 93.6 %reduce-scatter.14.cloned.1.call-done = f32[1,48,2304]{2,1,0:T(8,128)} async-done(((f32[1,768,2304]{2,1,0:T(8,128)}), f32[1,48,2304]{2,1,0:T(8,128)}) %reduce-scatter.14.cloned.1.call-update) | async-done | bytes 442384 | tf_op jit(solution)/shard_map/reduce_scatter | solution.py:340
  826.8 115.4 %reduce-scatter.18.cloned.1.call-done = f32[1,48,3072]{2,1,0:T(8,128)} async-done(((f32[1,768,3072]{2,1,0:T(8,128)}), f32[1,48,3072]{2,1,0:T(8,128)}) %reduce-scatter.18.cloned.1.call-update) | async-done | bytes 589840 | tf_op jit(solution)/shard_map/reduce_scatter | solution.py:342
  942.2 115.5 %reduce-scatter.20.cloned.1.call-done = f32[1,192,768]{2,1,0:T(8,128)} async-done(((f32[1,3072,768]{2,1,0:T(8,128)}), f32[1,192,768]{2,1,0:T(8,128)}) %reduce-scatter.20.cloned.1.call-update) | async-done | bytes 589840 | tf_op jit(solution)/shard_map/reduce_scatter | solution.py:343
  (456 shorter events, 102.8 us)
Async XLA Ops:
  7.2 48.1 %copy-start.151 = (u32[32]{0:T(128)S(1)}, u32[32]{0:T(128)}, u32[]{:S(2)}) copy-start(u32[32]{0:T(128)} %constant.279) | copy-start | bytes 388
  7.2 28.2 %copy-start.146 = (bf16[1,4,48]{2,1,0:T(4,128)(2,1)S(1)}, bf16[1,4,48]{2,1,0:T(4,128)(2,1)}, u32[]{:S(2)}) copy-start(bf16[1,4,48]{2,1,0:T(4,128)(2,1)} %param.26) | copy-start | bytes 1156
  7.2 48.0 %copy-start.147 = (bf16[1,192]{1,0:T(2,128)(2,1)S(1)}, bf16[1,192]{1,0:T(2,128)(2,1)}, u32[]{:S(2)}) copy-start(bf16[1,192]{1,0:T(2,128)(2,1)} %param.27) | copy-start | bytes 1156
  7.2 82.3 %copy-start.148 = (s32[256]{0:T(256)S(1)}, s32[256]{0:T(256)}, u32[]{:S(2)}) copy-start(s32[256]{0:T(256)} %param.20) | copy-start | bytes 3076
  7.2 84.8 %all-gather.7.cloned.1.call-start = ((), (), s32[]{:S(2)}) async-start(), calls=%async_computation.8 | async-start | bytes 1253376 | tf_op jit(solution)/shard_map/all_gather | solution.py:284
  8.0 200.4 %copy-start.59 = (bf16[256,768]{1,0:T(8,128)(2,1)S(1)}, bf16[256,768]{1,0:T(8,128)(2,1)}, u32[]{:S(2)}) copy-start(bf16[256,768]{1,0:T(8,128)(2,1)} %param.18) | copy-start | bytes 1179652
  8.0 92.4 %all-gather.5.cloned.1.call-start = ((), (), s32[]{:S(2)}) async-start(), calls=%async_computation.7 | async-start | bytes 3760128 | tf_op jit(solution)/shard_map/all_gather | solution.py:283
  8.7 145.8 %all-gather.9.cloned.1.call-start = ((), (), s32[]{:S(2)}) async-start(), calls=%async_computation.9 | async-start | bytes 5013504 | tf_op jit(solution)/shard_map/all_gather | solution.py:285
  9.4 198.9 %all-gather.11.cloned.1.call-start = ((), (), s32[]{:S(2)}) async-start(), calls=%async_computation.10 | async-start | bytes 5013504 | tf_op jit(solution)/shard_map/all_gather | solution.py:286
  10.0 539.6 %reduce-scatter.22.cloned.1.call-start = ((), (), s32[]{:S(2)}) async-start(), calls=%async_computation.15 | async-start | bytes 417792
  55.2 153.1 %copy-start.101 = (bf16[1,4,768]{2,1,0:T(4,128)(2,1)}, bf16[1,4,768]{2,1,0:T(4,128)(2,1)S(1)}, u32[]{:S(2)}) copy-start(bf16[1,4,768]{2,1,0:T(4,128)(2,1)S(1)} %copy.197) | copy-start | bytes 18436
  90.1 118.3 %copy-start.138 = (s32[128]{0:T(128)}, s32[128]{0:T(128)S(1)}, u32[]{:S(2)}) copy-start(s32[128]{0:T(128)S(1)} %get-tuple-element.841) | copy-start | bytes 1540
  90.1 118.3 %copy-start.142 = (s32[1,128]{1,0:T(1,128)}, s32[1,128]{1,0:T(1,128)S(1)}, u32[]{:S(2)}) copy-start(s32[1,128]{1,0:T(1,128)S(1)} %get-tuple-element.838) | copy-start | bytes 1540
  91.3 140.0 %copy-start.99 = (f32[768]{0:T(1024)}, f32[768]{0:T(1024)S(1)}, u32[]{:S(2)}) copy-start(f32[768]{0:T(1024)S(1)} %get-tuple-element.726) | copy-start | bytes 9220
  91.3 144.4 %copy-start.94 = (f32[768]{0:T(1024)}, f32[768]{0:T(1024)S(1)}, u32[]{:S(2)}) copy-start(f32[768]{0:T(1024)S(1)} %get-tuple-element.724) | copy-start | bytes 9220
  223.8 10.2 copy-start.28
  223.8 10.2 copy-start.91
  223.8 10.2 copy-start.149
  223.8 6.1 collective-permute-start
  225.8 8.9 copy-start.109
  231.0 166.6 %copy-start.10 = (bf16[128,768]{1,0:T(8,128)(2,1)}, bf16[128,768]{1,0:T(8,128)(2,1)S(1)}, u32[]{:S(2)}) copy-start(bf16[128,768]{1,0:T(8,128)(2,1)S(1)} %get-tuple-element.744) | copy-start | bytes 589828
  239.3 149.6 %copy-start.8 = (f32[128,3072]{1,0:T(8,128)}, f32[128,3072]{1,0:T(8,128)S(1)}, u32[]{:S(2)}) copy-start(f32[128,3072]{1,0:T(8,128)S(1)} %convolution_add_fusion.6) | copy-start | bytes 4718596
  240.3 10.6 copy-start.102
  240.3 10.6 copy-start.143
  242.2 8.7 collective-permute-start.1
  276.3 100.7 %copy-start.14 = (f32[12,128,128]{1,2,0:T(8,128)S(1)}, f32[12,128,128]{1,2,0:T(8,128)}, u32[]{:S(2)}) copy-start(f32[12,128,128]{1,2,0:T(8,128)} %copy-done.13) | copy-start | bytes 2359300
  276.4 100.7 %copy-start.104 = (f32[12,128]{1,0:T(8,128)S(1)}, f32[12,128]{1,0:T(8,128)}, u32[]{:S(2)}) copy-start(f32[12,128]{1,0:T(8,128)} %copy-done.103) | copy-start | bytes 18436
  276.4 99.2 %collective-permute-start.2 = (bf16[128,768]{1,0:T(8,128)(2,1)}, bf16[128,768]{1,0:T(8,128)(2,1)S(1)}, u32[]{:S(2)}, u32[]{:S(2)}) collective-permute-start(bf16[128,768]{1,0:T(8,128)(2,1)} %get-tuple-element.342), channel_id=1, source_target_pairs={{16,0},{17,1},{18,2},{19,3},{20,4},{21,5},{22,6},{23,7},{24,8},{25... | collective-permute-start | bytes 589832 | tf_op jit(solution)/shard_map/ppermute | solution.py:24
  279.6 98.6 %copy-start.40 = (bf16[128,768]{0,1:T(8,128)(2,1)S(1)}, bf16[128,768]{0,1:T(8,128)(2,1)}, u32[]{:S(2)}) copy-start(bf16[128,768]{0,1:T(8,128)(2,1)} %copy-done.39) | copy-start | bytes 589828
  376.5 27.9 %copy-start.18 = (bf16[128,768]{1,0:T(8,128)(2,1)}, bf16[128,768]{1,0:T(8,128)(2,1)S(1)}, u32[]{:S(2)}) copy-start(bf16[128,768]{1,0:T(8,128)(2,1)S(1)} %get-tuple-element.740) | copy-start | bytes 589828
  398.6 7.7 copy-start.70
  398.6 7.7 copy-start.92
  398.6 7.7 copy-start.139
  398.7 7.7 collective-permute-start.3
  406.6 10.2 copy-start.93
  407.3 8.7 copy-start.20
  422.5 16.9 %copy-start.7 = (bf16[768,2304]{1,0:T(8,128)(2,1)S(1)}, bf16[768,2304]{1,0:T(8,128)(2,1)}, u32[]{:S(2)}) copy-start(bf16[768,2304]{1,0:T(8,128)(2,1)} %get-tuple-element.270) | copy-start | bytes 10616836 | tf_op jit(solution)/shard_map/cond
  449.1 8.0 copy-start.22
  465.7 9.7 copy-start.16
  480.5 9.7 copy-start.106
  480.5 9.7 copy-start.107
  480.5 9.7 copy-start.108
  492.2 112.2 %reduce-scatter.24.cloned.1.call-start = ((), (), s32[]{:S(2)}) async-start(), calls=%async_computation.16 | async-start | bytes 417792
  494.0 172.6 %reduce-scatter.26.cloned.1.call-start = ((), (), s32[]{:S(2)}) async-start(), calls=%async_computation.17 | async-start | bytes 1671168
  496.5 236.6 %reduce-scatter.16.cloned.1.call-start = ((), (), s32[]{:S(2)}) async-start(), calls=%async_computation.12 | async-start | bytes 2506752 | tf_op jit(solution)/shard_map/reduce_scatter | solution.py:341
  501.3 325.5 %reduce-scatter.14.cloned.1.call-start = ((), (), s32[]{:S(2)}) async-start(), calls=%async_computation.11 | async-start | bytes 7520256 | tf_op jit(solution)/shard_map/reduce_scatter | solution.py:340
  517.8 424.4 %reduce-scatter.18.cloned.1.call-start = ((), (), s32[]{:S(2)}) async-start(), calls=%async_computation.13 | async-start | bytes 10027008 | tf_op jit(solution)/shard_map/reduce_scatter | solution.py:342
  531.3 526.4 %reduce-scatter.20.cloned.1.call-start = ((), (), s32[]{:S(2)}) async-start(), calls=%async_computation.14 | async-start | bytes 10027008 | tf_op jit(solution)/shard_map/reduce_scatter | solution.py:343
  (95 other events, 270.9 us)
Sparse Core Ops, SparseCore 0:
  10.3 42.0 all-gather.6
  54.7 45.6 all-gather.4
  102.6 51.7 all-gather.8
  156.6 51.6 all-gather.10
  492.3 53.6 reduce-scatter.21
  549.3 55.0 reduce-scatter.23
  608.1 58.5 reduce-scatter.25
  671.0 62.1 reduce-scatter.15
  737.8 88.9 reduce-scatter.13
  831.3 110.8 reduce-scatter.17
  946.9 110.8 reduce-scatter.19
where the time goes:
time: 1080 us; the launch traced here: 1060 us
  waiting for transfers between devices  726 us (67%)
  local copies, waits for them, and re-layouts  90.5 us (8%)
  matrix products  79 us (7%)
  blocking collectives  75.8 us (7%)
  other arithmetic  65.4 us (6%)
  between operations  16.2 us (2%)
    unnamed x14, waiting for transfers between devices  117 us
    reduce_scatter x1, waiting for transfers between devices, on_device(): lax.psum_scatter(total[3][None], 'dp', scatter_dimension=1, tiled=True)  116 us
    reduce_scatter x1, waiting for transfers between devices, on_device(): lax.psum_scatter(total[2][None], 'dp', scatter_dimension=1, tiled=True)  115 us
    ppermute x4, waiting for transfers between devices, shifted(): lax.ppermute(value, axis, [(source, source + steps) for source in range(i...  103 us
    reduce_scatter x1, waiting for transfers between devices, on_device(): lax.psum_scatter(total[0][None], 'dp', scatter_dimension=1, tiled=True)  93.6 us
    reduce_scatter x1, waiting for transfers between devices, on_device(): lax.psum_scatter(total[1][None], 'dp', scatter_dimension=1, tiled=True)  65 us
    all_gather x1, waiting for transfers between devices, on_device(): lax.all_gather(up_weight, 'dp', axis=1, tiled=True)  54.1 us
    all_gather x1, waiting for transfers between devices, on_device(): lax.all_gather(down_weight, 'dp', axis=1, tiled=True)  53.8 us
  transfers between devices with their start and end apart: 15, of which 12 were waited for; matrix products, arithmetic and copies ran while one was open for 7% of the time, Pallas kernels for 0%

commit v1 on v0

--- a/solution.py
+++ b/solution.py
@@ -9,7 +9,8 @@
 FF = 3072
 HEAD = 64
 ROT = 16
-MICRO = 2
+PACK = 128
+LANES = 128
 
 
 EPS = 1e-05
@@ -141,28 +142,6 @@
         activation_output,
     )
     return (result, saved_state)
-
-
-def blank_forward(rows):
-    heads = D // HEAD
-    single = jnp.float32
-    half = jnp.bfloat16
-    saved_state = (
-        jnp.zeros((rows, D), single),
-        jnp.zeros((rows, 1), single),
-        jnp.zeros((rows, D), half),
-        jnp.zeros((rows, D), single),
-        jnp.zeros((rows, 1), single),
-        jnp.zeros((rows, D), half),
-        jnp.zeros((1, rows, heads, HEAD), half),
-        jnp.zeros((1, rows, heads, HEAD), half),
-        jnp.zeros((1, rows, heads, HEAD), half),
-        jnp.zeros((1, heads, rows, 1), single),
-        jnp.zeros((rows, D), half),
-        jnp.zeros((rows, FF), single),
-        jnp.zeros((rows, FF), half),
-    )
-    return (jnp.zeros((rows, D), half), saved_state)
 
 
 def backward(saved_state, upstream, seg, weights):
@@ -186,7 +165,9 @@
     shape = (packs, width, D // HEAD, HEAD)
     norm_pairs = norm_pairs.astype(jnp.float32)
     upf = upstream.astype(jnp.float32)
-    d_down = jnp.dot(activation_output.T, upstream, preferred_element_type=jnp.float32)
+    d_down = jnp.dot(activation_output.T, upstream, preferred_element_type=jnp.float32).astype(
+        jnp.bfloat16
+    )
     dgelu = jnp.dot(upstream, wdown.T, preferred_element_type=jnp.float32)
     slope = 0.5 * (1.0 + lax.erf(hidden_rows * HALF_ROOT)) + hidden_rows * INV_ROOT_TAU * jnp.exp(
         -0.5 * hidden_rows * hidden_rows
@@ -232,29 +213,6 @@
     return (grad_in, (d_qkv, d_out, d_up, d_down, d_norm, d_bias, d_upbias))
 
 
-def blank_backward(rows, weights):
-    grads = tuple((jnp.zeros(piece.shape, jnp.float32) for piece in weights))
-    return (jnp.zeros((rows, D), jnp.bfloat16), grads)
-
-
-def forward_step(active, x_now, seg, weights):
-    if active is None:
-        return forward(x_now, seg, weights)
-    return lax.cond(
-        active, lambda: forward(x_now, seg, weights), lambda: blank_forward(x_now.shape[0])
-    )
-
-
-def backward_step(active, saved_state, upstream, seg, weights):
-    if active is None:
-        return backward(saved_state, upstream, seg, weights)
-    return lax.cond(
-        active,
-        lambda: backward(saved_state, upstream, seg, weights),
-        lambda: blank_backward(upstream.shape[0], weights),
-    )
-
-
 def send_forward(result):
     return shifted(result, "section", 1)
 
@@ -276,92 +234,49 @@
     up_bias,
 ):
     is_first = lax.axis_index("section") == 0
-    is_second = jnp.logical_not(is_first)
-    micro = MICRO
-    pack = inputs.shape[0] // micro
-    gathered = (
-        lax.all_gather(qkv_weight, "dp", axis=1, tiled=True),
-        lax.all_gather(out_weight, "dp", axis=1, tiled=True),
-        lax.all_gather(up_weight, "dp", axis=1, tiled=True),
-        lax.all_gather(down_weight, "dp", axis=1, tiled=True),
-        lax.all_gather(norm_params, "dp", axis=2, tiled=True),
-        lax.all_gather(bias_params, "dp", axis=2, tiled=True),
-        lax.all_gather(up_bias, "dp", axis=1, tiled=True),
-    )
-    weights = tuple((piece[0] for piece in gathered))
-
-    def rows_of(array, index):
-        return array[index * pack : (index + 1) * pack]
-
-    arrived = jnp.zeros((pack, D), jnp.bfloat16)
-    outs = []
-    kept = []
-    seg_list = []
-    for step in range(micro + 1):
-        lead = min(step, micro - 1)
-        trail = max(step - 1, 0)
-        x_now = jnp.where(is_first, rows_of(inputs, lead), arrived)
-        seg = jnp.where(is_first, rows_of(segments, lead), rows_of(segments, trail)).reshape(
-            1, pack
-        )
-        active = is_first if step == 0 else is_second if step == micro else None
-        result, saved_state = forward_step(active, x_now, seg, weights)
-        if step < micro:
-            arrived = send_forward(result)
-        outs.append(result)
-        kept.append(saved_state)
-        seg_list.append(seg)
-    regathered = (
-        lax.all_gather(qkv_weight, "dp", axis=1, tiled=True),
-        lax.all_gather(out_weight, "dp", axis=1, tiled=True),
-        lax.all_gather(up_weight, "dp", axis=1, tiled=True),
-        lax.all_gather(down_weight, "dp", axis=1, tiled=True),
-        lax.all_gather(norm_params, "dp", axis=2, tiled=True),
-        lax.all_gather(bias_params, "dp", axis=2, tiled=True),
-        lax.all_gather(up_bias, "dp", axis=1, tiled=True),
-    )
-    back_weights = tuple((piece[0] for piece in regathered))
-    returned = jnp.zeros((pack, D), jnp.bfloat16)
-    grads_in = []
-    total = None
-    owned = None
-    for step in range(micro + 1):
-        index = micro - step
-        upstream = jnp.where(is_first, returned, rows_of(cotangent, max(micro - 1 - step, 0)))
-        active = is_second if step == 0 else is_first if step == micro else None
-        grad_in, grads = backward_step(active, kept[index], upstream, seg_list[index], back_weights)
-        if step < micro:
-            returned = send_back(grad_in)
-        grads_in.append(grad_in)
-        total = (
-            grads if total is None else tuple((left + right for left, right in zip(total, grads)))
-        )
-    owned = (
-        lax.psum_scatter(total[0][None], "dp", scatter_dimension=1, tiled=True),
-        lax.psum_scatter(total[1][None], "dp", scatter_dimension=1, tiled=True),
-        lax.psum_scatter(total[2][None], "dp", scatter_dimension=1, tiled=True),
-        lax.psum_scatter(total[3][None], "dp", scatter_dimension=1, tiled=True),
-        lax.psum_scatter(total[4][None], "dp", scatter_dimension=2, tiled=True),
-        lax.psum_scatter(total[5][None], "dp", scatter_dimension=2, tiled=True),
-        lax.psum_scatter(total[6][None], "dp", scatter_dimension=1, tiled=True),
-    )
-    layer_out = jnp.concatenate(
-        [jnp.where(is_first, outs[j], outs[j + 1]) for j in range(micro)], axis=0
-    )
-    input_grad = jnp.concatenate(
-        [jnp.where(is_first, grads_in[micro - j], grads_in[micro - 1 - j]) for j in range(micro)],
-        axis=0,
-    )
+    rows = qkv_weight.shape[1]
+    tokens = inputs.shape[0]
+    seg = segments.reshape(tokens // PACK, PACK)
+
+    small = jnp.concatenate(
+        [norm_params[0].T, bias_params[0].T, up_bias.reshape(rows, FF // D)], axis=1
+    )
+    small_width = small.shape[1]
+    small = jnp.pad(small, ((0, 0), (0, LANES - small_width)))
+    packed = jnp.concatenate([small, qkv_weight[0], out_weight[0], up_weight[0]], axis=1)
+    cuts = [LANES, LANES + 3 * D, LANES + 4 * D]
+    packed = lax.all_gather(packed, "dp", axis=0, tiled=True)
+    wdown = lax.all_gather(down_weight[0], "dp", axis=0, tiled=True)
+    small, wqkv, wout, wup = jnp.split(packed, cuts, axis=1)
+    small = small[:, :small_width].T
+    weights = (wqkv, wout, wup, wdown, small[:4], small[4:8], small[8:].T.reshape(FF))
+
+    lead, _ = forward(inputs, seg, weights)
+    x = jnp.where(is_first, inputs, send_forward(lead))
+    layer_out, saved_state = forward(x, seg, weights)
+    trail, _ = backward(saved_state, cotangent, seg, weights)
+    upstream = jnp.where(is_first, send_back(trail), cotangent)
+    input_grad, grads = backward(saved_state, upstream, seg, weights)
+    d_qkv, d_out, d_up, d_down, d_norm, d_bias, d_upbias = grads
+
+    d_down = lax.psum_scatter(d_down, "dp", scatter_dimension=0, tiled=True)
+    d_small = jnp.concatenate([d_norm.T, d_bias.T, d_upbias.reshape(D, FF // D)], axis=1)
+    d_small = jnp.pad(d_small, ((0, 0), (0, LANES - small_width)))
+    owned = jnp.concatenate(
+        [piece.astype(jnp.bfloat16) for piece in (d_small, d_qkv, d_out, d_up)], axis=1
+    )
+    owned = lax.psum_scatter(owned, "dp", scatter_dimension=0, tiled=True).astype(jnp.float32)
+    d_small, d_qkv, d_out, d_up = jnp.split(owned, cuts, axis=1)
     return (
         layer_out[None],
         input_grad[None],
-        owned[0],
-        owned[1],
-        owned[2],
-        owned[3],
-        owned[4],
-        owned[5],
-        owned[6],
+        d_qkv[None],
+        d_out[None],
+        d_up[None],
+        d_down.astype(jnp.float32)[None],
+        d_small[:, :4].T[None],
+        d_small[:, 4:8].T[None],
+        d_small[:, 8:small_width].reshape(1, -1),
     )
 
 

time: 1080 us -> 448 us (0.41); the launches traced: 1060 us -> 445 us
  waiting for transfers between devices: 726 us -> 256 us
  blocking collectives: 75.8 us -> 0 us
  local copies, waits for them, and re-layouts: 90.5 us -> 38.8 us
  other arithmetic: 65.4 us -> 22.8 us
  matrix products: 79 us -> 106 us
    reduce_scatter x4 -> x2, waiting for transfers between devices: 390 us -> 112 us  [the longest x1 112 us: on_device(): lax.psum_scatter(owned, 'dp', scatter_dimension=0, tiled=True)]
    unnamed x14 -> x4, waiting for transfers between devices: 117 us -> 0.74 us
    ppermute x4 -> x2, waiting for transfers between devices: 103 us -> 17.7 us  [shifted(): lax.ppermute(value, axis, [(source, source + steps) for source in range(i...]
    all_gather x2 -> x0, blocking collectives: 43.7 us -> none  [the longest x1 24.3 us: on_device(): lax.all_gather(norm_params, 'dp', axis=2, tiled=True)]
    broadcast_in_dim x7 -> x1, other arithmetic: 39.7 us -> 1.81 us  [on_device(): d_down.astype(jnp.float32)[None]]
    squeeze x1 -> x0, blocking collectives: 32.1 us -> none  [on_device(): weights = tuple((piece[0] for piece in gathered))]
    cond x88 -> x0, local copies, waits for them, and re-layouts: 32.1 us -> none  [the longest x4 29.5 us: backward_step(): lax.cond(active, lambda: backward(saved_state, upstream, seg, weights), l...]
    another operation x24 -> x3, local copies, waits for them, and re-layouts: 26 us -> 2.45 us
  transfers between devices with their start and end apart: 15 -> 6, of which waited for: 12 -> 5; matrix products, arithmetic and copies ran while one was open for 7% -> 20% of each run, Pallas kernels for 0% -> 0%
where the time goes in v1:
time: 448 us; the launch traced here: 445 us
  waiting for transfers between devices  256 us (57%)
  matrix products  106 us (24%)
  local copies, waits for them, and re-layouts  38.8 us (9%)
  other arithmetic  22.8 us (5%)
  between operations  15.4 us (3%)
  starting transfers between devices  5.24 us (1%)
    reduce_scatter x1, waiting for transfers between devices, on_device(): lax.psum_scatter(owned, 'dp', scatter_dimension=0, tiled=True)  112 us
    all_gather x1, waiting for transfers between devices, on_device(): packed = lax.all_gather(packed, 'dp', axis=0, tiled=True)  81.9 us
    all_gather x1, waiting for transfers between devices, on_device(): wdown = lax.all_gather(down_weight[0], 'dp', axis=0, tiled=True)  43.3 us
    dot_general x2, matrix products, backward(): jnp.dot(dhidden_low, wup.T, preferred_element_type=jnp.float32)  24.3 us
    dot_general x12, matrix products, mix(): return jnp.einsum(form, left, right, preferred_element_type=jnp.float32)  24.2 us
    ppermute x2, waiting for transfers between devices, shifted(): lax.ppermute(value, axis, [(source, source + steps) for source in range(i...  17.7 us
    dot_general x2, matrix products, forward(): jnp.dot(activation_output, wdown, preferred_element_type=jnp.float32)  10.5 us
    dot_general x2, matrix products, backward(): jnp.dot(dqkv, wqkv.T, preferred_element_type=jnp.float32)  9.24 us
  transfers between devices with their start and end apart: 6, of which 5 were waited for; matrix products, arithmetic and copies ran while one was open for 20% of the time, Pallas kernels for 0%

profile of v1, /device:TPU:0, one launch (start us, length us, event | category | flops | bytes accessed | tf_op | source)
XLA Modules:
  0.0 444.6 jit_solution(882424135889421488)
XLA Ops:
  9.0 1.9 fusion.166
  14.1 81.9 %all-gather.4.cloned.1.call-done = bf16[768,6272]{1,0:T(8,128)(2,1)} async-done(((bf16[48,6272]{1,0:T(8,128)(2,1)}), bf16[768,6272]{1,0:T(8,128)(2,1)}) %all-gather.4.cloned.1.call-update) | async-done | bytes 9633808 | tf_op jit(solution)/shard_map/all_gather | solution.py:248
  97.3 1.5 slice_reduce_fusion.3
  98.9 3.2 fusion.34
  106.5 43.3 %all-gather.6.cloned.1.call-done = bf16[1,3072,768]{2,1,0:T(8,128)(2,1)} async-done(((bf16[1,192,768]{2,1,0:T(8,128)(2,1)}), bf16[1,3072,768]{2,1,0:T(8,128)(2,1)}) %all-gather.6.cloned.1.call-update) | async-done | bytes 4718608 | tf_op jit(solution)/shard_map/all_gather | solution.py:249
  149.8 6.7 %fusion.76 = f32[256,768]{1,0:T(8,128)S(1)} fusion(bf16[1,3072,768]{2,1,0:T(8,128)(2,1)} %all-gather.6.cloned.1.call-done, bf16[768,6272]{1,0:T(8,128)(2,1)} %all-gather.4.cloned.1.call-done, f32[3072]{0:T(1024)S(1)} %reshape.254, bf16[256,768]{1,0:T(8,128)(2,1)S(1)} %copy-done, f32[768]{0:T(1024)S(1)} %get-tuple-element.62, ...), kind=kOutput, calls=%fused_computation.70 | convolution fusion | flops 2422013952 | bytes 10640384 | tf_op jit(solution)/shard_map/dot_general | solution.py:127
  156.6 1.9 fusion.82
  158.5 3.7 collective-permute-start
  162.1 1.8 fusion.88
  164.0 6.6 %collective-permute-done = bf16[256,768]{1,0:T(8,128)(2,1)S(1)} collective-permute-done((bf16[256,768]{1,0:T(8,128)(2,1)S(1)}, bf16[256,768]{1,0:T(8,128)(2,1)S(1)}, u32[]{:S(2)}, u32[]{:S(2)}) %collective-permute-start) | collective-permute-done | bytes 393248 | tf_op jit(solution)/shard_map/ppermute | solution.py:25
  171.9 3.2 fusion.32
  182.1 1.6 fusion.210
  183.7 3.8 fusion.60
  187.5 3.7 fusion.63
  195.8 6.5 %multiply_convert_fusion = (bf16[256,3072]{1,0:T(8,128)(2,1)}, f32[256,3072]{1,0:T(8,128)}) fusion(f32[3072]{0:T(1024)S(1)} %copy-done.58, bf16[768,6272]{1,0:T(8,128)(2,1)} %all-gather.4.cloned.1.call-done, bf16[256,768]{1,0:T(8,128)(2,1)S(1)} %get-tuple-element.72, f32[256]{0:T(256)S(1)} %copy-done.40, f32[256]{0:T(256)S(1)} %copy-done.35, ...), kind=kOutput, calls=%fused_computation.23 | convolution fusion | flops 1213857792 | bytes 9850880 | tf_op jit(solution)/shard_map/dot_general | solution.py:123
  202.4 19.6 %fusion.73 = f32[256,768]{1,0:T(8,128)} fusion(bf16[768,6272]{1,0:T(8,128)(2,1)} %all-gather.4.cloned.1.call-done, bf16[256,768]{1,0:T(8,128)(2,1)S(1)} %copy-done.5, bf16[1,3072,768]{2,1,0:T(8,128)(2,1)} %all-gather.6.cloned.1.call-done, f32[768]{0:T(1024)S(1)} %get-tuple-element.135, f32[256,3072]{1,0:T(8,128)} %get-tuple-element.129), kind=kOutput, calls=%fused_computation.69 | convolution fusion | flops 2423980032 | bytes 13765632 | tf_op jit(solution)/shard_map/dot_general | solution.py:178
  221.9 4.0 fusion.238
  226.5 1.4 collective-permute-start.1
  227.9 11.1 %collective-permute-done.1 = bf16[256,768]{1,0:T(8,128)(2,1)S(1)} collective-permute-done((bf16[256,768]{1,0:T(8,128)(2,1)S(1)}, bf16[256,768]{1,0:T(8,128)(2,1)S(1)}, u32[]{:S(2)}, u32[]{:S(2)}) %collective-permute-start.1) | collective-permute-done | bytes 393248 | tf_op jit(solution)/shard_map/ppermute | solution.py:25
  239.8 3.7 convolution_convert_fusion
  243.9 1.2 copy.180
  245.7 8.0 %fusion.248 = (bf16[3072]{0:T(1024)(128)(2,1)}, bf16[256,3072]{1,0:T(8,128)(2,1)}) fusion(f32[256,3072]{1,0:T(8,128)} %get-tuple-element.129, bf16[256,768]{1,0:T(8,128)(2,1)S(1)} %get-tuple-element.70, bf16[1,3072,768]{2,1,0:T(8,128)(2,1)} %all-gather.6.cloned.1.call-done), kind=kOutput, calls=%fused_computation.320 | convolution fusion | flops 1216607232 | bytes 9836544 | tf_op jit(solution)/shard_map/dot_general | solution.py:171
  253.7 1.8 reshape.252
  255.5 2.6 convolution_convert_fusion.4
  258.1 1.9 copy.190
  260.0 1.8 convert_element_type.205
  261.8 3.0 fusion.241
  264.8 1.4 stack.42
  266.2 1.4 copy.199
  267.6 2.6 fusion.207
  270.2 3.9 fusion.57
  274.2 1.1 slice.304
  275.3 3.4 fusion.54
  278.7 1.1 slice.255
  279.8 1.1 subtract_convert_fusion
  283.3 4.7 %fusion.22 = f32[256,768]{1,0:T(8,128)S(1)} fusion(bf16[768,6272]{1,0:T(8,128)(2,1)} %all-gather.4.cloned.1.call-done, bf16[256,3072]{1,0:T(8,128)(2,1)} %get-tuple-element.133), kind=kOutput, calls=%fused_computation.26 | convolution fusion | flops 1207959552 | bytes 7077888 | tf_op jit(solution)/shard_map/dot_general | solution.py:178
  288.0 5.2 %fusion.147 = (bf16[768]{0:T(1024)(128)(2,1)S(1)}, f32[256]{0:T(256)}, f32[256]{0:T(256)}, bf16[768]{0:T(1024)(128)(2,1)S(1)}, bf16[768]{0:T(1024)(128)(2,1)S(1)...) fusion(bf16[256,768]{1,0:T(8,128)(2,1)S(1)} %get-tuple-element.72, ...), kind=kOutput, calls=%fused_computation.143 | convolution fusion | flops 909307904 | bytes 6703104 | tf_op jit(solution)/shard_map/dot_general | solution.py:199
  295.6 1.4 fusion.217
  297.0 2.7 convolution_convert_fusion.2
  299.8 1.6 convolution_convert_fusion.1
  301.3 6.9 %pad_maximum_fusion = bf16[768,6272]{1,0:T(8,128)(2,1)} fusion(bf16[768,3072]{1,0:T(8,128)(2,1)S(1)} %convolution_convert_fusion.1, bf16[768,768]{1,0:T(8,128)(2,1)S(1)} %copy.202, bf16[768,2304]{1,0:T(8,128)(2,1)S(1)} %convolution_convert_fusion.2, bf16[768,128]{1,0:T(8,128)(2,1)S(1)} %fusion.217), kind=kLoop, calls=%fused_computation.2 | loop fusion | flops 38535168 | bytes 19267584 | tf_op jit(solution)/shard_map/concatenate | solution.py:265
  308.3 1.4 copy-done.2
  309.7 3.7 fusion.79
  313.5 2.7 fusion.85
  316.3 1.3 fusion.203
  317.5 1.8 bitcast_convert_fusion
  319.3 112.2 %reduce-scatter.3.cloned.1.call-done = bf16[48,6272]{1,0:T(8,128)(2,1)} async-done(((bf16[768,6272]{1,0:T(8,128)(2,1)}), bf16[48,6272]{1,0:T(8,128)(2,1)}) %reduce-scatter.3.cloned.1.call-update) | async-done | bytes 602128 | tf_op jit(solution)/shard_map/reduce_scatter | solution.py:268
  431.5 1.1 convert_element_type.212
  (265 shorter events, 35.1 us)
Async XLA Ops:
  7.2 4.6 %copy-start.56 = (s32[256]{0:T(256)S(1)}, s32[256]{0:T(256)}, u32[]{:S(2)}) copy-start(s32[256]{0:T(256)} %param.12) | copy-start | bytes 3076
  7.2 5.0 %copy-start = (bf16[256,768]{1,0:T(8,128)(2,1)S(1)}, bf16[256,768]{1,0:T(8,128)(2,1)}, u32[]{:S(2)}) copy-start(bf16[256,768]{1,0:T(8,128)(2,1)} %param.10) | copy-start | bytes 1179652
  7.2 88.8 %all-gather.4.cloned.1.call-start = ((), (), s32[]{:S(2)}) async-start(), calls=%async_computation.2 | async-start | bytes 10235904 | tf_op jit(solution)/shard_map/all_gather | solution.py:248
  11.0 138.8 %all-gather.6.cloned.1.call-start = ((), (), s32[]{:S(2)}) async-start(), calls=%async_computation.5 | async-start | bytes 5013504 | tf_op jit(solution)/shard_map/all_gather | solution.py:249
  11.7 305.8 %reduce-scatter.5.cloned.1.call-start = ((), (), s32[]{:S(2)}) async-start(), calls=%async_computation.4 | async-start | bytes 5013504 | tf_op jit(solution)/shard_map/reduce_scatter | solution.py:262
  12.6 86.3 %copy-start.66 = (f32[256]{0:T(256)}, f32[256]{0:T(256)S(1)}, u32[]{:S(2)}) copy-start(f32[256]{0:T(256)S(1)} %add_rsqrt_fusion.1) | copy-start | bytes 3076
  13.4 91.2 %copy-start.30 = (f32[2,128,8]{1,2,0:T(8,128)}, f32[2,128,8]{1,2,0:T(8,128)S(1)}, u32[]{:S(2)}) copy-start(f32[2,128,8]{1,2,0:T(8,128)S(1)} %get-tuple-element.121) | copy-start | bytes 24580
  97.3 52.5 %copy-start.57 = (f32[3072]{0:T(1024)}, f32[3072]{0:T(1024)S(1)}, u32[]{:S(2)}) copy-start(f32[3072]{0:T(1024)S(1)} %reshape.254) | copy-start | bytes 36868
  98.9 3.3 copy-start.50
  98.9 3.3 copy-start.52
  98.9 51.0 %copy-start.24 = (f32[768]{0:T(1024)}, f32[768]{0:T(1024)S(1)}, u32[]{:S(2)}) copy-start(f32[768]{0:T(1024)S(1)} %get-tuple-element.136) | copy-start | bytes 9220
  98.9 50.9 %copy-start.64 = (f32[768]{0:T(1024)}, f32[768]{0:T(1024)S(1)}, u32[]{:S(2)}) copy-start(f32[768]{0:T(1024)S(1)} %get-tuple-element.62) | copy-start | bytes 9220
  98.9 57.7 %copy-start.62 = (f32[768]{0:T(1024)}, f32[768]{0:T(1024)S(1)}, u32[]{:S(2)}) copy-start(f32[768]{0:T(1024)S(1)} %get-tuple-element.61) | copy-start | bytes 9220
  98.9 72.2 %copy-start.27 = (f32[768]{0:T(1024)}, f32[768]{0:T(1024)S(1)}, u32[]{:S(2)}) copy-start(f32[768]{0:T(1024)S(1)} %get-tuple-element.134) | copy-start | bytes 9220
  105.7 44.1 %copy-start.67 = (f32[256]{0:T(256)S(1)}, f32[256]{0:T(256)}, u32[]{:S(2)}) copy-start(f32[256]{0:T(256)} %copy-done.66) | copy-start | bytes 3076
  156.6 5.5 %copy-start.4 = (bf16[256,768]{1,0:T(8,128)(2,1)S(1)}, bf16[256,768]{1,0:T(8,128)(2,1)}, u32[]{:S(2)}) copy-start(bf16[256,768]{1,0:T(8,128)(2,1)} %param.11) | copy-start | bytes 1179652
  158.5 12.1 %collective-permute-start = (bf16[256,768]{1,0:T(8,128)(2,1)S(1)}, bf16[256,768]{1,0:T(8,128)(2,1)S(1)}, u32[]{:S(2)}, u32[]{:S(2)}) collective-permute-start(bf16[256,768]{1,0:T(8,128)(2,1)S(1)} %fusion.82), channel_id=1, source_target_pairs={{0,16},{1,17},{2,18},{3,19},{4,20},{5,21},{6,22},{7,23},{8,24},{9,... | collective-permute-start | bytes 1179656 | tf_op jit(solution)/shard_map/ppermute | solution.py:25
  171.9 3.2 copy-start.51
  171.9 3.2 copy-start.53
  195.8 6.5 %copy-start.5 = (bf16[256,768]{1,0:T(8,128)(2,1)S(1)}, bf16[256,768]{1,0:T(8,128)(2,1)}, u32[]{:S(2)}) copy-start(bf16[256,768]{1,0:T(8,128)(2,1)} %param.11) | copy-start | bytes 1179652
  221.9 4.1 copy-start.13
  221.9 4.1 copy-start.36
  221.9 4.1 copy-start.41
  226.0 13.1 %copy-start.6 = (bf16[256,768]{1,0:T(8,128)(2,1)S(1)}, bf16[256,768]{1,0:T(8,128)(2,1)}, u32[]{:S(2)}) copy-start(bf16[256,768]{1,0:T(8,128)(2,1)} %param.11) | copy-start | bytes 1179652
  226.0 13.8 %copy-start.1 = (bf16[256,3072]{1,0:T(8,128)(2,1)S(1)}, bf16[256,3072]{1,0:T(8,128)(2,1)}, u32[]{:S(2)}) copy-start(bf16[256,3072]{1,0:T(8,128)(2,1)} %get-tuple-element.128) | copy-start | bytes 4718596
  226.5 12.6 %collective-permute-start.1 = (bf16[256,768]{1,0:T(8,128)(2,1)S(1)}, bf16[256,768]{1,0:T(8,128)(2,1)S(1)}, u32[]{:S(2)}, u32[]{:S(2)}) collective-permute-start(bf16[256,768]{1,0:T(8,128)(2,1)S(1)} %fusion.131), channel_id=1, source_target_pairs={{16,0},{17,1},{18,2},{19,3},{20,4},{21,5},{22,6},{23,7},{24,8},{25... | collective-permute-start | bytes 1179656 | tf_op jit(solution)/shard_map/ppermute | solution.py:25
  243.5 188.0 %reduce-scatter.3.cloned.1.call-start = ((), (), s32[]{:S(2)}) async-start(), calls=%async_computation.3 | async-start | bytes 10235904 | tf_op jit(solution)/shard_map/reduce_scatter | solution.py:268
  266.2 4.0 copy-start.23
  266.2 4.0 copy-start.33
  270.2 5.1 %copy-start.21 = (bf16[2,128,12,48]{1,3,2,0:T(8,128)(2,1)S(1)}, bf16[2,128,12,48]{1,3,2,0:T(8,128)(2,1)}, u32[]{:S(2)}) copy-start(bf16[2,128,12,48]{1,3,2,0:T(8,128)(2,1)} %copy-done.20) | copy-start | bytes 884740
  270.2 5.1 %copy-start.45 = (bf16[2,128,12,8]{1,3,2,0:T(8,128)(2,1)S(1)}, bf16[2,128,12,8]{1,3,2,0:T(8,128)(2,1)}, u32[]{:S(2)}) copy-start(bf16[2,128,12,8]{1,3,2,0:T(8,128)(2,1)} %copy-done.44) | copy-start | bytes 147460
  270.2 5.1 %copy-start.47 = (bf16[2,128,12,8]{1,3,2,0:T(8,128)(2,1)S(1)}, bf16[2,128,12,8]{1,3,2,0:T(8,128)(2,1)}, u32[]{:S(2)}) copy-start(bf16[2,128,12,8]{1,3,2,0:T(8,128)(2,1)} %copy-done.46) | copy-start | bytes 147460
  283.3 4.7 %copy-start.3 = (bf16[256,2304]{0,1:T(8,128)(2,1)}, bf16[256,2304]{0,1:T(8,128)(2,1)S(1)}, u32[]{:S(2)}) copy-start(bf16[256,2304]{0,1:T(8,128)(2,1)S(1)} %bitcast_dynamic-update-slice_fusion) | copy-start | bytes 3538948
  283.3 4.7 %copy-start.37 = (f32[256]{0:T(256)S(1)}, f32[256]{0:T(256)}, u32[]{:S(2)}) copy-start(f32[256]{0:T(256)} %copy-done.34) | copy-start | bytes 3076
  283.3 4.7 %copy-start.42 = (f32[256]{0:T(256)S(1)}, f32[256]{0:T(256)}, u32[]{:S(2)}) copy-start(f32[256]{0:T(256)} %copy-done.39) | copy-start | bytes 3076
  288.0 5.2 %copy-start.10 = (f32[256,768]{1,0:T(8,128)}, f32[256,768]{1,0:T(8,128)S(1)}, u32[]{:S(2)}) copy-start(f32[256,768]{1,0:T(8,128)S(1)} %fusion.22) | copy-start | bytes 2359300
  288.0 6.1 %copy-start.7 = (bf16[2,128,12,64]{1,0,3,2:T(2,128)(2,1)S(1)}, bf16[2,128,12,64]{1,0,3,2:T(2,128)(2,1)}, u32[]{:S(2)}) copy-start(bf16[2,128,12,64]{1,0,3,2:T(2,128)(2,1)} %copy.180) | copy-start | bytes 1179652
  296.9 2.8 copy-start.8
  296.9 2.8 copy-start.26
  296.9 2.8 copy-start.38
  297.0 2.8 copy-start.43
  309.7 3.8 copy-start.63
  313.4 2.8 copy-start.71
  313.4 2.7 copy-start.70
  313.4 2.8 copy-start.69
  313.5 2.8 copy-start.68
  313.5 2.8 copy-start.11
  313.5 2.8 copy-start.12
  (30 other events, 35.9 us)
Sparse Core Ops, SparseCore 0:
  11.1 84.8 all-gather.3
  98.3 51.5 all-gather.5
  243.6 73.1 reduce-scatter.4
  320.8 110.6 reduce-scatter.2
